TPU v7x, 256 devices: a whole 4x4x8 slice. The times are simulated.
256 devices in a mesh: row: 32 (over z_hi, x, core), col: 8 (over z_lo, y).
Axes of the slice: x: 4, y: 4, z: 8 (z_hi: 4, z_lo: 2; z = z_hi * 2 + z_lo), core: 2. Of those that a mesh axis runs over, the one named last changes fastest.
Arguments:
- density_factor: bfloat16 [6144, 512], P('row', 'col'), may hold values from -0.25 to 0.25
- hole_factor: bfloat16 [6144, 512], P('row', 'col'), may hold values from -0.25 to 0.25
- ph_factor: bfloat16 [6144, 512], P('row', 'col'), may hold values from -0.25 to 0.25
- hamiltonian: bfloat16 [6144, 6144], P('row', 'col'), as said below
- multiplier_q: bfloat16 [6144, 6144], P('row', 'col'), as said below
- multiplier_g: bfloat16 [6144, 6144], P('row', 'col'), as said below
- ph_perm: int32 [6144], replicated, may hold values from 0 to 6143, as said below
- block_lengths: int32 [48], replicated, may hold values from 1 to 256, 6144 in all
Outputs:
- grad_density: float32 [6144, 512], P('row', 'col')
- grad_hole: float32 [6144, 512], P('row', 'col')
- grad_ph: float32 [6144, 512], P('row', 'col')
Inputs may be any that keep to these rules, and one draw needn't show every extreme that they name: `ph_perm`: a permutation of the rows; each aligned block of 192 entries holds exactly 6 values from each aligned range of 192 rows. `block_lengths`: the lengths sum to 6144. `hamiltonian`: symmetric. `multiplier_q`: symmetric. `multiplier_g`: symmetric.
All inputs are finite; a program needn't handle non-finite values.
Results may differ from a plain program's by a relative error of at most 0.00035.
The roundings to bfloat16 on the way count: a program that leaves them out, or rounds other values in their place, can miss the bound.
Values may be sent and summed in bfloat16 or wider, within the bound.
No kernel may reach another device: no remote copies, remote signals or barrier semaphores. Data moves between devices by JAX's collectives and lax.ppermute only.
A program may use at most 64 MiB of HBM per device.

v0:
```python
import jax
import jax.numpy as jnp
from jax import lax
from jax.sharding import PartitionSpec as P

shift_value = 2.0
penalty = 2.5


def block_means(values, lengths):
    offsets = jnp.cumsum(lengths)
    positions = jnp.arange(values.shape[0], dtype=jnp.int32)
    segment = jnp.sum((positions[:, None] >= offsets[None, :]).astype(jnp.int32), axis=1)
    member = (segment[:, None] == jnp.arange(lengths.shape[0], dtype=jnp.int32)[None, :]).astype(
        jnp.float32
    )
    means = jnp.sum(member * values[:, None], axis=0) / lengths.astype(jnp.float32)
    return jnp.sum(member * means[None, :], axis=1)


def contract_rows(left, right):
    return lax.dot_general(
        left, right, (((1,), (1,)), ((), ())), preferred_element_type=jnp.float32
    )


def local(
    density_factor,
    hole_factor,
    ph_factor,
    hamiltonian,
    multiplier_q,
    multiplier_g,
    ph_perm,
    block_lengths,
):
    groups = lax.axis_size("row")
    row_index = lax.axis_index("row")
    col_index = lax.axis_index("col")
    block = density_factor.shape[0]
    rank_part = density_factor.shape[1]
    width = multiplier_q.shape[1]
    sends = block // groups
    row_ids = row_index * block + jnp.arange(block, dtype=jnp.int32)
    col_ids = col_index * width + jnp.arange(width, dtype=jnp.int32)
    on_diag = row_ids[:, None] == col_ids[None, :]
    density_sq = jnp.sum(jnp.square(density_factor.astype(jnp.float32)), axis=1)
    ph_sq = jnp.sum(jnp.square(ph_factor.astype(jnp.float32)), axis=1)
    mult_diag = jnp.sum(jnp.where(on_diag, multiplier_g.astype(jnp.float32), 0.0), axis=1)
    density_sq, ph_sq, mult_diag = lax.psum((density_sq, ph_sq, mult_diag), "col")
    density_all, ph_all, mult_all = (
        lax.all_gather(density_sq, "row", axis=0, tiled=True),
        lax.all_gather(ph_sq, "row", axis=0, tiled=True),
        lax.all_gather(mult_diag, "row", axis=0, tiled=True),
    )
    shifted = 2.0 * block_means(density_all, block_lengths)
    shifted_ph = jnp.take(shifted, ph_perm)
    weight_diag = mult_all + penalty * (shifted_ph - jnp.take(density_all, ph_perm) - ph_all)
    weight_pair = jnp.zeros_like(weight_diag).at[ph_perm].set(weight_diag)
    scaling = 2.0 * block_means(weight_pair, block_lengths)
    scale_rows = lax.dynamic_slice_in_dim(scaling, row_index * block, block)
    shift_rows = lax.dynamic_slice_in_dim(shifted_ph, row_index * block, block)
    table = ph_perm.reshape(groups, block)
    source = table // block
    mine = lax.dynamic_index_in_dim(source, row_index, 0, keepdims=False)
    member = (mine[:, None] == jnp.arange(groups, dtype=jnp.int32)[None, :]).astype(jnp.int32)
    earlier = jnp.cumsum(member, axis=0) - member
    slot = mine * sends + jnp.sum(earlier * member, axis=1)
    slot_back = jnp.argsort(slot)
    position = jnp.arange(block, dtype=jnp.int32)[None, :]
    ranked = jnp.where(source == row_index, position, block + position)
    chosen = jnp.argsort(ranked, axis=1)[:, :sends]
    anchor = (jnp.take_along_axis(table, chosen, axis=1) - row_index * block).reshape(block)
    anchor_back = jnp.argsort(anchor)
    pair_local = jnp.concatenate([density_factor, hole_factor], axis=1)
    outgoing = jnp.take(density_factor, anchor, axis=0)
    incoming = lax.all_to_all(outgoing, "row", split_axis=0, concat_axis=0, tiled=True)
    density_ph = jnp.take(incoming, slot, axis=0)
    ph_local = jnp.concatenate([density_ph, ph_factor], axis=1)
    pair_whole, ph_whole = (
        lax.all_gather(pair_local, "row", axis=0, tiled=True),
        lax.all_gather(ph_local, "row", axis=0, tiled=True),
    )
    pair_rows = pair_whole
    ph_rows = ph_whole
    gram_cols = lax.psum_scatter(
        jnp.concatenate(
            [contract_rows(pair_rows, pair_local), contract_rows(ph_rows, ph_local)], axis=1
        ),
        "col",
        scatter_dimension=0,
        tiled=True,
    )
    resid_q = jnp.where(on_diag, shift_value, 0.0) - gram_cols[:, :block].T
    resid_g = jnp.where(on_diag, shift_rows[:, None], 0.0) - gram_cols[:, block:].T
    weight_q = (multiplier_q.astype(jnp.float32) + penalty * resid_q).astype(jnp.bfloat16)
    weight_g = (multiplier_g.astype(jnp.float32) + penalty * resid_g).astype(jnp.bfloat16)
    weight_q, weight_g = (weight_q, weight_g)
    pair_rows = pair_whole
    ph_rows = ph_whole
    energy = jnp.dot(
        lax.all_gather(hamiltonian, "col", axis=1, tiled=True),
        pair_rows[:, :rank_part],
        preferred_element_type=jnp.float32,
    )
    pair_acc = jnp.dot(
        lax.all_gather(weight_q, "col", axis=1, tiled=True),
        pair_rows,
        preferred_element_type=jnp.float32,
    )
    ph_acc = jnp.dot(
        lax.all_gather(weight_g, "col", axis=1, tiled=True),
        ph_rows,
        preferred_element_type=jnp.float32,
    )
    pair_grad = jnp.concatenate(
        [2.0 * energy - 2.0 * pair_acc[:, :rank_part], -2.0 * pair_acc[:, rank_part:]], axis=1
    )
    outgoing_back = jnp.take(ph_acc[:, :rank_part], slot_back, axis=0)
    returned = lax.all_to_all(outgoing_back, "row", split_axis=0, concat_axis=0, tiled=True)
    returned = jnp.take(returned, anchor_back, axis=0)
    grad_density = (
        pair_grad[:, :rank_part]
        + 2.0 * scale_rows[:, None] * density_factor.astype(jnp.float32)
        - 2.0 * returned
    )
    grad_hole = pair_grad[:, rank_part:]
    grad_ph = -2.0 * ph_acc[:, rank_part:]
    return (grad_density, grad_hole, grad_ph)


def solution(mesh):
    return jax.shard_map(
        local,
        mesh=mesh,
        in_specs=(
            P("row", "col"),
            P("row", "col"),
            P("row", "col"),
            P("row", "col"),
            P("row", "col"),
            P("row", "col"),
            P(),
            P(),
        ),
        out_specs=(P("row", "col"), P("row", "col"), P("row", "col")),
        check_vma=False,
    )
```

profile of v0, /device:TPU:2, one launch (start us, length us, event | category | flops | bytes accessed | tf_op | source)
XLA Modules:
  0.0 627.2 jit_solution(385054818816971866)
XLA Ops:
  7.2 0.9 copy.38
  8.1 0.9 copy.39
  9.7 0.8 reshape.102
  10.6 3.7 sort.48
  14.4 1.9 gather_fusion
  16.6 0.8 gather_fusion.1
  18.3 11.6 %all-to-all-start = ((bf16[32,2,192]{2,1,0:T(2,128)(2,1)}), bf16[32,2,192]{2,1,0:T(2,128)(2,1)S(1)}, u32[]{:S(2)}, u32[]{:S(2)}) async-start(bf16[32,2,192]{2,1,0:T(2,128)(2,1)} %reshape.214), calls=%async_computation | async-start | bytes 65536 | tf_op jit(solution)/shard_map/all_to_all | solution.py:77
  31.1 7.4 %all-to-all-done = bf16[32,2,192]{2,1,0:T(2,128)(2,1)S(1)} async-done(((bf16[32,2,192]{2,1,0:T(2,128)(2,1)}), bf16[32,2,192]{2,1,0:T(2,128)(2,1)S(1)}, u32[]{:S(2)}, u32[]{:S(2)}) %all-to-all-start) | async-done | bytes 24608 | tf_op jit(solution)/shard_map/all_to_all | solution.py:77
  38.6 0.8 gather_fusion.2
  41.9 19.4 %all-reduce.5 = (f32[192]{0:T(256)S(1)}, f32[192]{0:T(256)S(1)}, f32[192]{0:T(256)S(1)}) all-reduce(f32[192]{0:T(256)S(1)} %fusion.25, f32[192]{0:T(256)S(1)} %fusion.22, f32[192]{0:T(256)S(1)} %multiply_reduce_fusion), channel_id=1, replica_groups=mesh['row'=32,'col'=8] {'col'}, use_global_device_ids=true, to_apply=%region_10.12 | all-reduce | flops 576 | bytes 4608 | tf_op jit(solution)/shard_map/psum | solution.py:50
  62.9 3.5 all-gather.6.cloned.1.call-done
  66.4 4.3 fusion.35
  70.7 49.3 %all-gather.10.cloned.1.call-done = bf16[6144,128]{1,0:T(8,128)(2,1)} async-done(((bf16[192,128]{1,0:T(8,128)(2,1)}), bf16[6144,128]{1,0:T(8,128)(2,1)}) %all-gather.10.cloned.1.call-update) | async-done | bytes 1572880 | tf_op jit(solution)/shard_map/all_gather | solution.py:82
  120.0 2.3 fusion.36
  122.8 4.7 pad_maximum_fusion
  128.7 242.1 %all-reduce.8.cloned.1.call-done = (f32[6144]{0:T(1024)}, f32[6144]{0:T(1024)}, f32[6144]{0:T(1024)}) async-done(((f32[6144]{0:T(1024)}, f32[6144]{0:T(1024)}, f32[6144]{0:T(1024)}), (f32[6144]{0:T(1024)}, f32[6144]{0:T(1024)}, f32[6144]{0:T(1024)})) %all-reduce.8.cloned.1.call-update) | async-done | bytes 73744
  370.8 28.4 %gather_fusion.4 = f32[6144]{0:T(1024)S(1)} fusion(f32[6144]{0:T(1024)} %get-tuple-element.24, s32[6144]{0:T(1024)S(1)} %get-tuple-element.43), kind=kCustom, calls=%fused_computation.4.clone | custom fusion | bytes 73728 | tf_op jit(solution)/shard_map/jit(_take)/gather | solution.py:58
  399.8 34.3 %gather_fusion.3 = f32[6144]{0:T(1024)S(1)} fusion(f32[6144]{0:T(1024)S(1)} %broadcast_multiply_fusion, s32[6144]{0:T(1024)S(1)} %get-tuple-element.43), kind=kCustom, calls=%fused_computation.1.clone | custom fusion | bytes 73728 | tf_op jit(solution)/shard_map/jit(_take)/gather | solution.py:57
  434.2 45.5 %reduce-scatter.2.cloned.1.call-done = f32[768,384]{0,1:T(8,128)} async-done(((f32[6144,384]{0,1:T(8,128)}), f32[768,384]{0,1:T(8,128)}) %reduce-scatter.2.cloned.1.call-update) | async-done | bytes 1179664 | tf_op jit(solution)/shard_map/reduce_scatter | solution.py:86
  479.8 2.4 fusion.21
  483.5 3.2 sort.49
  486.7 3.2 sort.50
  489.9 23.2 %scatter_custom_fusion = f32[6144]{0:T(1024)S(1)} fusion(s32[6144]{0:T(1024)S(1)} %get-tuple-element.42, f32[6144]{0:T(1024)S(1)} %get-tuple-element.30, f32[]{:T(128)} %constant.68.clone.1), kind=kCustom, calls=%fused_computation.76 | custom fusion | bytes 24580 | tf_op jit(solution)/shard_map/scatter | solution.py:59
  513.7 12.0 %all-gather.14.cloned.1.call-done = bf16[192,6144]{1,0:T(8,128)(2,1)} async-done(((bf16[192,768]{1,0:T(8,128)(2,1)}), bf16[192,6144]{1,0:T(8,128)(2,1)}) %all-gather.14.cloned.1.call-update) | async-done | bytes 2359312 | tf_op jit(solution)/shard_map/all_gather | solution.py:112
  525.7 2.4 fusion.38
  529.1 0.7 reshape.216
  529.8 9.0 %all-to-all-start.1 = ((f32[32,1,384]{2,1,0:T(1,128)}), f32[32,1,384]{2,1,0:T(1,128)S(1)}, u32[]{:S(2)}, u32[]{:S(2)}) async-start(f32[32,1,384]{2,1,0:T(1,128)} %reshape.216), calls=%async_computation.2 | async-start | bytes 98304 | tf_op jit(solution)/shard_map/all_to_all | solution.py:120
  538.8 32.1 %all-gather.12.cloned.1.call-done = bf16[192,6144]{1,0:T(8,128)(2,1)} async-done(((bf16[192,768]{1,0:T(8,128)(2,1)}), bf16[192,6144]{1,0:T(8,128)(2,1)}) %all-gather.12.cloned.1.call-update) | async-done | bytes 2359312 | tf_op jit(solution)/shard_map/all_gather | solution.py:107
  570.9 2.4 fusion.37
  575.4 0.8 reduce.3
  577.1 40.1 %all-gather.8.cloned.1.call-done = bf16[192,6144]{1,0:T(8,128)(2,1)} async-done(((bf16[192,768]{1,0:T(8,128)(2,1)}), bf16[192,6144]{1,0:T(8,128)(2,1)}) %all-gather.8.cloned.1.call-update) | async-done | bytes 2359312 | tf_op jit(solution)/shard_map/all_gather | solution.py:102
  617.2 3.1 fusion.14
  (136 shorter events, 14.7 us)
Async XLA Ops:
  7.2 59.2 %all-gather.6.cloned.1.call-start = ((), (), s32[]{:S(2)}) async-start(), calls=%async_computation.3 | async-start | bytes 1622016 | tf_op jit(solution)/shard_map/all_gather | solution.py:81
  14.4 16.6 %copy-start.10 = (bf16[192,64]{0,1:T(8,128)(2,1)S(1)}, bf16[192,64]{0,1:T(8,128)(2,1)}, u32[]{:S(2)}) copy-start(bf16[192,64]{0,1:T(8,128)(2,1)} %param.16) | copy-start | bytes 73732
  16.3 24.0 %copy-start.19 = (u32[256]{0:T(256)S(1)}, u32[256]{0:T(256)}, u32[]{:S(2)}) copy-start(u32[256]{0:T(256)} %constant.123) | copy-start | bytes 3076
  16.3 25.3 %copy-start.7 = (bf16[192,64]{0,1:T(8,128)(2,1)S(1)}, bf16[192,64]{0,1:T(8,128)(2,1)}, u32[]{:S(2)}) copy-start(bf16[192,64]{0,1:T(8,128)(2,1)} %param.14) | copy-start | bytes 73732
  16.3 25.3 %copy-start.4 = (bf16[192,768]{1,0:T(8,128)(2,1)S(1)}, bf16[192,768]{1,0:T(8,128)(2,1)}, u32[]{:S(2)}) copy-start(bf16[192,768]{1,0:T(8,128)(2,1)} %param.19) | copy-start | bytes 884740
  16.4 50.0 %copy-start.5 = (bf16[192,128]{1,0:T(8,128)(2,1)S(1)}, bf16[192,128]{1,0:T(8,128)(2,1)}, u32[]{:S(2)}) copy-start(bf16[192,128]{1,0:T(8,128)(2,1)} %pad_maximum_fusion.1) | copy-start | bytes 147460
  18.3 20.2 %all-to-all-start = ((bf16[32,2,192]{2,1,0:T(2,128)(2,1)}), bf16[32,2,192]{2,1,0:T(2,128)(2,1)S(1)}, u32[]{:S(2)}, u32[]{:S(2)}) async-start(bf16[32,2,192]{2,1,0:T(2,128)(2,1)} %reshape.214), calls=%async_computation | async-start | bytes 65536 | tf_op jit(solution)/shard_map/all_to_all | solution.py:77
  29.9 90.1 %all-gather.10.cloned.1.call-start = ((), (), s32[]{:S(2)}) async-start(), calls=%async_computation.5 | async-start | bytes 1622016 | tf_op jit(solution)/shard_map/all_gather | solution.py:82
  40.3 330.5 %all-reduce.8.cloned.1.call-start = ((), (), s32[]{:S(2)}) async-start(), calls=%async_computation.9 | async-start | bytes 147456
  41.6 20.6 %copy-start.16 = (s32[192]{0:T(256)}, s32[192]{0:T(256)S(1)}, u32[]{:S(2)}) copy-start(s32[192]{0:T(256)S(1)} %iota_add_fusion.2) | copy-start | bytes 2308
  61.6 0.6 copy-start.12
  61.9 0.6 copy-start.13
  62.2 0.6 copy-start.11
  62.8 57.2 %copy-start.6 = (bf16[192,128]{1,0:T(8,128)(2,1)S(1)}, bf16[192,128]{1,0:T(8,128)(2,1)}, u32[]{:S(2)}) copy-start(bf16[192,128]{1,0:T(8,128)(2,1)} %pad_maximum_fusion.2) | copy-start | bytes 147460
  62.8 417.0 %reduce-scatter.2.cloned.1.call-start = ((), (), s32[]{:S(2)}) async-start(), calls=%async_computation.6 | async-start | bytes 10616832 | tf_op jit(solution)/shard_map/reduce_scatter | solution.py:86
  120.0 2.8 copy-start.1
  127.5 0.7 copy-start.18
  127.5 1.2 copy-start.9
  127.5 398.2 %all-gather.14.cloned.1.call-start = ((), (), s32[]{:S(2)}) async-start(), calls=%async_computation.8 | async-start | bytes 2654208 | tf_op jit(solution)/shard_map/all_gather | solution.py:112
  370.8 28.4 %copy-start = (f32[6144]{0:T(1024)S(1)}, f32[6144]{0:T(1024)}, u32[]{:S(2)}) copy-start(f32[6144]{0:T(1024)} %get-tuple-element.24) | copy-start | bytes 73732
  399.7 34.3 %copy-start.14 = (f32[6144]{0:T(1024)S(1)}, f32[6144]{0:T(1024)}, u32[]{:S(2)}) copy-start(f32[6144]{0:T(1024)} %get-tuple-element.25) | copy-start | bytes 73732
  399.8 34.3 %copy-start.15 = (f32[6144]{0:T(1024)S(1)}, f32[6144]{0:T(1024)}, u32[]{:S(2)}) copy-start(f32[6144]{0:T(1024)} %get-tuple-element.26) | copy-start | bytes 73732
  399.8 80.0 %copy-start.8 = (bf16[192,768]{1,0:T(8,128)(2,1)S(1)}, bf16[192,768]{1,0:T(8,128)(2,1)}, u32[]{:S(2)}) copy-start(bf16[192,768]{1,0:T(8,128)(2,1)} %param.18) | copy-start | bytes 884740
  399.8 80.0 %copy-start.17 = (s32[192]{0:T(256)S(1)}, s32[192]{0:T(256)}, u32[]{:S(2)}) copy-start(s32[192]{0:T(256)} %copy-done.16) | copy-start | bytes 2308
  434.2 91.5 %copy-start.3 = (bf16[6144,128]{1,0:T(8,128)(2,1)S(1)}, bf16[6144,128]{1,0:T(8,128)(2,1)}, u32[]{:S(2)}) copy-start(bf16[6144,128]{1,0:T(8,128)(2,1)} %all-gather.10.cloned.1.call-done) | copy-start | bytes 4718596
  482.2 88.7 %all-gather.12.cloned.1.call-start = ((), (), s32[]{:S(2)}) async-start(), calls=%async_computation.7 | async-start | bytes 2654208 | tf_op jit(solution)/shard_map/all_gather | solution.py:107
  482.7 134.5 %all-gather.8.cloned.1.call-start = ((), (), s32[]{:S(2)}) async-start(), calls=%async_computation.4 | async-start | bytes 2654208 | tf_op jit(solution)/shard_map/all_gather | solution.py:102
  528.1 42.7 %copy-start.2 = (bf16[6144,128]{1,0:T(8,128)(2,1)S(1)}, bf16[6144,128]{1,0:T(8,128)(2,1)}, u32[]{:S(2)}) copy-start(bf16[6144,128]{1,0:T(8,128)(2,1)} %all-gather.6.cloned.1.call-done) | copy-start | bytes 4718596
  529.8 45.1 %all-to-all-start.1 = ((f32[32,1,384]{2,1,0:T(1,128)}), f32[32,1,384]{2,1,0:T(1,128)S(1)}, u32[]{:S(2)}, u32[]{:S(2)}) async-start(f32[32,1,384]{2,1,0:T(1,128)} %reshape.216), calls=%async_computation.2 | async-start | bytes 98304 | tf_op jit(solution)/shard_map/all_to_all | solution.py:120
Sparse Core Ops, SparseCore 0:
  11.1 55.2 all-gather.5
  69.5 50.4 all-gather.9
  123.4 247.3 all-reduce.7
  373.4 106.3 reduce-scatter.1
  482.3 43.3 all-gather.13
  527.5 43.3 all-gather.11
  572.8 44.3 all-gather.7
where the time goes:
time: 628 us; the launch traced here: 627 us
  waiting for transfers between devices  433 us (69%)
  local copies, waits for them, and re-layouts  101 us (16%)
  other arithmetic  22.5 us (4%)
  starting transfers between devices  20.9 us (3%)
  blocking collectives  19.4 us (3%)
  between operations  15.3 us (2%)
  matrix products  14.6 us (2%)
    unnamed x8, waiting for transfers between devices  243 us
    all_gather x1, waiting for transfers between devices, local(): lax.all_gather(ph_local, 'row', axis=0, tiled=True)  49.3 us
    reduce_scatter x1, waiting for transfers between devices, local(): lax.psum_scatter(jnp.concatenate([contract_rows(pair_rows, pair_local), c...  45.5 us
    all_gather x1, waiting for transfers between devices, local(): lax.all_gather(hamiltonian, 'col', axis=1, tiled=True)  40.1 us
    gather x1, local copies, waits for them, and re-layouts, local(): shifted_ph = jnp.take(shifted, ph_perm)  34.3 us
    all_gather x1, waiting for transfers between devices, local(): lax.all_gather(weight_q, 'col', axis=1, tiled=True)  32.1 us
    gather x1, local copies, waits for them, and re-layouts, local(): jnp.take(density_all, ph_perm)  28.4 us
    scatter x1, local copies, waits for them, and re-layouts, local(): weight_pair = jnp.zeros_like(weight_diag).at[ph_perm].set(weight_diag)  23.2 us
  transfers between devices with their start and end apart: 9, of which 8 were waited for; matrix products, arithmetic and copies ran while one was open for 20% of the time, Pallas kernels for 0%

commit v1 on v0

--- a/solution.py
+++ b/solution.py
@@ -104,7 +104,9 @@
         preferred_element_type=jnp.float32,
     )
     pair_acc = jnp.dot(
-        lax.all_gather(weight_q, "col", axis=1, tiled=True),
+        jnp.concatenate(
+            lax.all_to_all(jnp.stack([weight_q] * lax.axis_size("col")), "col", 0, 0), axis=1
+        ),
         pair_rows,
         preferred_element_type=jnp.float32,
     )

time: 628 us -> 602 us (0.959)
  waiting for transfers between devices: 433 us -> 397 us
  local copies, waits for them, and re-layouts: 101 us -> 108 us
    all_gather x1 -> x0, waiting for transfers between devices: 32.1 us -> none  [local(): lax.all_gather(weight_q, 'col', axis=1, tiled=True)]
    all_gather x1, waiting for transfers between devices: 40.1 us -> 22.2 us  [local(): lax.all_gather(hamiltonian, 'col', axis=1, tiled=True)]
    unnamed x8 -> x7, waiting for transfers between devices: 243 us -> 243 us
  transfers between devices with their start and end apart: 9 -> 9, of which waited for: 8 -> 9; matrix products, arithmetic and copies ran while one was open for 20% -> 22% of each run, Pallas kernels for 0% -> 0%
where the time goes in v1:
time: 602 us; the launch traced here: 601 us
  waiting for transfers between devices  397 us (66%)
  local copies, waits for them, and re-layouts  108 us (18%)
  starting transfers between devices  24.2 us (4%)
  other arithmetic  22.5 us (4%)
  blocking collectives  19.4 us (3%)
  between operations  15.3 us (3%)
  matrix products  14.6 us (2%)
    unnamed x7, waiting for transfers between devices  243 us
    all_gather x1, waiting for transfers between devices, local(): lax.all_gather(ph_local, 'row', axis=0, tiled=True)  49.2 us
    reduce_scatter x1, waiting for transfers between devices, local(): lax.psum_scatter(jnp.concatenate([contract_rows(pair_rows, pair_local), c...  45.5 us
    gather x1, local copies, waits for them, and re-layouts, local(): shifted_ph = jnp.take(shifted, ph_perm)  34.3 us
    gather x1, local copies, waits for them, and re-layouts, local(): jnp.take(density_all, ph_perm)  28.4 us
    scatter x1, local copies, waits for them, and re-layouts, local(): weight_pair = jnp.zeros_like(weight_diag).at[ph_perm].set(weight_diag)  23.2 us
    all_gather x1, waiting for transfers between devices, local(): lax.all_gather(hamiltonian, 'col', axis=1, tiled=True)  22.2 us
    psum x1, blocking collectives, local(): lax.psum((density_sq, ph_sq, mult_diag), 'col')  19.4 us
  transfers between devices with their start and end apart: 9, of which 9 were waited for; matrix products, arithmetic and copies ran while one was open for 22% of the time, Pallas kernels for 0%

profile of v1, /device:TPU:2, one launch (start us, length us, event | category | flops | bytes accessed | tf_op | source)
XLA Modules:
  0.0 600.8 jit_solution(16489496962214085795)
XLA Ops:
  7.2 0.9 copy.39
  8.1 0.9 copy.40
  10.6 3.7 sort.48
  14.4 1.9 gather_fusion
  18.3 11.6 %all-to-all-start = ((bf16[32,2,192]{2,1,0:T(2,128)(2,1)}), bf16[32,2,192]{2,1,0:T(2,128)(2,1)S(1)}, u32[]{:S(2)}, u32[]{:S(2)}) async-start(bf16[32,2,192]{2,1,0:T(2,128)(2,1)} %reshape.224), calls=%async_computation | async-start | bytes 65536 | tf_op jit(solution)/shard_map/all_to_all | solution.py:77
  31.1 7.4 %all-to-all-done = bf16[32,2,192]{2,1,0:T(2,128)(2,1)S(1)} async-done(((bf16[32,2,192]{2,1,0:T(2,128)(2,1)}), bf16[32,2,192]{2,1,0:T(2,128)(2,1)S(1)}, u32[]{:S(2)}, u32[]{:S(2)}) %all-to-all-start) | async-done | bytes 24608 | tf_op jit(solution)/shard_map/all_to_all | solution.py:77
  41.9 19.4 %all-reduce.5 = (f32[192]{0:T(256)S(1)}, f32[192]{0:T(256)S(1)}, f32[192]{0:T(256)S(1)}) all-reduce(f32[192]{0:T(256)S(1)} %fusion.25, f32[192]{0:T(256)S(1)} %fusion.22, f32[192]{0:T(256)S(1)} %multiply_reduce_fusion), channel_id=1, replica_groups=mesh['row'=32,'col'=8] {'col'}, use_global_device_ids=true, to_apply=%region_10.12 | all-reduce | flops 576 | bytes 4608 | tf_op jit(solution)/shard_map/psum | solution.py:50
  62.9 3.5 all-gather.5.cloned.1.call-done
  66.4 4.4 fusion.35
  70.8 49.2 %all-gather.9.cloned.1.call-done = bf16[6144,128]{1,0:T(8,128)(2,1)} async-done(((bf16[192,128]{1,0:T(8,128)(2,1)}), bf16[6144,128]{1,0:T(8,128)(2,1)}) %all-gather.9.cloned.1.call-update) | async-done | bytes 1572880 | tf_op jit(solution)/shard_map/all_gather | solution.py:82
  120.0 2.3 fusion.36
  122.8 4.7 pad_maximum_fusion
  128.7 242.1 %all-reduce.8.cloned.1.call-done = (f32[6144]{0:T(1024)}, f32[6144]{0:T(1024)}, f32[6144]{0:T(1024)}) async-done(((f32[6144]{0:T(1024)}, f32[6144]{0:T(1024)}, f32[6144]{0:T(1024)}), (f32[6144]{0:T(1024)}, f32[6144]{0:T(1024)}, f32[6144]{0:T(1024)})) %all-reduce.8.cloned.1.call-update) | async-done | bytes 73744
  370.8 28.4 %gather_fusion.4 = f32[6144]{0:T(1024)S(1)} fusion(f32[6144]{0:T(1024)} %get-tuple-element.24, s32[6144]{0:T(1024)S(1)} %get-tuple-element.43), kind=kCustom, calls=%fused_computation.4.clone | custom fusion | bytes 73728 | tf_op jit(solution)/shard_map/jit(_take)/gather | solution.py:58
  399.8 34.3 %gather_fusion.3 = f32[6144]{0:T(1024)S(1)} fusion(f32[6144]{0:T(1024)S(1)} %broadcast_multiply_fusion, s32[6144]{0:T(1024)S(1)} %get-tuple-element.43), kind=kCustom, calls=%fused_computation.1.clone | custom fusion | bytes 73728 | tf_op jit(solution)/shard_map/jit(_take)/gather | solution.py:57
  434.2 45.5 %reduce-scatter.2.cloned.1.call-done = f32[768,384]{0,1:T(8,128)} async-done(((f32[6144,384]{0,1:T(8,128)}), f32[768,384]{0,1:T(8,128)}) %reduce-scatter.2.cloned.1.call-update) | async-done | bytes 1179664 | tf_op jit(solution)/shard_map/reduce_scatter | solution.py:86
  479.8 2.3 fusion.21
  482.1 1.6 stack.2
  483.7 3.6 all-to-all-start.1
  487.9 3.2 sort.49
  491.1 3.2 sort.50
  494.3 23.2 %scatter_custom_fusion = f32[6144]{0:T(1024)S(1)} fusion(s32[6144]{0:T(1024)S(1)} %get-tuple-element.42, f32[6144]{0:T(1024)S(1)} %get-tuple-element.30, f32[]{:T(128)} %constant.68.clone.1), kind=kCustom, calls=%fused_computation.76 | custom fusion | bytes 24580 | tf_op jit(solution)/shard_map/scatter | solution.py:59
  518.2 6.2 %all-to-all-done.1 = bf16[8,192,768]{2,1,0:T(8,128)(2,1)S(1)} async-done(((bf16[8,192,768]{2,1,0:T(8,128)(2,1)}), bf16[8,192,768]{2,1,0:T(8,128)(2,1)S(1)}, u32[]{:S(2)}, u32[]{:S(2)}) %all-to-all-start.1) | async-done | bytes 2359328 | tf_op jit(solution)/shard_map/all_to_all | solution.py:108
  524.4 1.4 copy-done.4
  525.8 3.5 copy.54
  529.4 15.6 %all-gather.11.cloned.1.call-done = bf16[192,6144]{1,0:T(8,128)(2,1)} async-done(((bf16[192,768]{1,0:T(8,128)(2,1)}), bf16[192,6144]{1,0:T(8,128)(2,1)}) %all-gather.11.cloned.1.call-update) | async-done | bytes 2359312 | tf_op jit(solution)/shard_map/all_gather | solution.py:114
  545.0 2.4 fusion.38
  549.1 8.7 %all-to-all-start.2 = ((f32[32,1,384]{2,1,0:T(1,128)}), f32[32,1,384]{2,1,0:T(1,128)S(1)}, u32[]{:S(2)}, u32[]{:S(2)}) async-start(f32[32,1,384]{2,1,0:T(1,128)} %reshape.226), calls=%async_computation.3 | async-start | bytes 98304 | tf_op jit(solution)/shard_map/all_to_all | solution.py:122
  557.8 2.4 fusion.37
  561.8 4.7 all-to-all-done.2
  568.6 22.2 %all-gather.7.cloned.1.call-done = bf16[192,6144]{1,0:T(8,128)(2,1)} async-done(((bf16[192,768]{1,0:T(8,128)(2,1)}), bf16[192,6144]{1,0:T(8,128)(2,1)}) %all-gather.7.cloned.1.call-update) | async-done | bytes 2359312 | tf_op jit(solution)/shard_map/all_gather | solution.py:102
  590.9 3.1 fusion.14
  (139 shorter events, 17.8 us)
Async XLA Ops:
  7.2 59.2 %all-gather.5.cloned.1.call-start = ((), (), s32[]{:S(2)}) async-start(), calls=%async_computation.4 | async-start | bytes 1622016 | tf_op jit(solution)/shard_map/all_gather | solution.py:81
  14.4 16.6 %copy-start.11 = (bf16[192,64]{0,1:T(8,128)(2,1)S(1)}, bf16[192,64]{0,1:T(8,128)(2,1)}, u32[]{:S(2)}) copy-start(bf16[192,64]{0,1:T(8,128)(2,1)} %param.16) | copy-start | bytes 73732
  16.3 24.0 %copy-start.20 = (u32[256]{0:T(256)S(1)}, u32[256]{0:T(256)}, u32[]{:S(2)}) copy-start(u32[256]{0:T(256)} %constant.123) | copy-start | bytes 3076
  16.3 25.3 %copy-start.8 = (bf16[192,64]{0,1:T(8,128)(2,1)S(1)}, bf16[192,64]{0,1:T(8,128)(2,1)}, u32[]{:S(2)}) copy-start(bf16[192,64]{0,1:T(8,128)(2,1)} %param.14) | copy-start | bytes 73732
  16.3 25.3 %copy-start.5 = (bf16[192,768]{1,0:T(8,128)(2,1)S(1)}, bf16[192,768]{1,0:T(8,128)(2,1)}, u32[]{:S(2)}) copy-start(bf16[192,768]{1,0:T(8,128)(2,1)} %param.19) | copy-start | bytes 884740
  16.4 50.0 %copy-start.6 = (bf16[192,128]{1,0:T(8,128)(2,1)S(1)}, bf16[192,128]{1,0:T(8,128)(2,1)}, u32[]{:S(2)}) copy-start(bf16[192,128]{1,0:T(8,128)(2,1)} %pad_maximum_fusion.1) | copy-start | bytes 147460
  18.3 20.2 %all-to-all-start = ((bf16[32,2,192]{2,1,0:T(2,128)(2,1)}), bf16[32,2,192]{2,1,0:T(2,128)(2,1)S(1)}, u32[]{:S(2)}, u32[]{:S(2)}) async-start(bf16[32,2,192]{2,1,0:T(2,128)(2,1)} %reshape.224), calls=%async_computation | async-start | bytes 65536 | tf_op jit(solution)/shard_map/all_to_all | solution.py:77
  29.9 90.1 %all-gather.9.cloned.1.call-start = ((), (), s32[]{:S(2)}) async-start(), calls=%async_computation.6 | async-start | bytes 1622016 | tf_op jit(solution)/shard_map/all_gather | solution.py:82
  40.3 330.5 %all-reduce.8.cloned.1.call-start = ((), (), s32[]{:S(2)}) async-start(), calls=%async_computation.9 | async-start | bytes 147456
  41.6 20.6 %copy-start.17 = (s32[192]{0:T(256)}, s32[192]{0:T(256)S(1)}, u32[]{:S(2)}) copy-start(s32[192]{0:T(256)S(1)} %iota_add_fusion.2) | copy-start | bytes 2308
  61.6 0.6 copy-start.13
  61.9 0.6 copy-start.14
  62.2 0.6 copy-start.12
  62.8 57.2 %copy-start.7 = (bf16[192,128]{1,0:T(8,128)(2,1)S(1)}, bf16[192,128]{1,0:T(8,128)(2,1)}, u32[]{:S(2)}) copy-start(bf16[192,128]{1,0:T(8,128)(2,1)} %pad_maximum_fusion.2) | copy-start | bytes 147460
  62.8 417.0 %reduce-scatter.2.cloned.1.call-start = ((), (), s32[]{:S(2)}) async-start(), calls=%async_computation.7 | async-start | bytes 10616832 | tf_op jit(solution)/shard_map/reduce_scatter | solution.py:86
  120.0 2.8 copy-start.1
  127.5 0.7 copy-start.19
  127.5 1.2 copy-start.10
  127.6 417.4 %all-gather.11.cloned.1.call-start = ((), (), s32[]{:S(2)}) async-start(), calls=%async_computation.8 | async-start | bytes 2654208 | tf_op jit(solution)/shard_map/all_gather | solution.py:114
  370.8 28.4 %copy-start = (f32[6144]{0:T(1024)S(1)}, f32[6144]{0:T(1024)}, u32[]{:S(2)}) copy-start(f32[6144]{0:T(1024)} %get-tuple-element.24) | copy-start | bytes 73732
  399.8 34.3 %copy-start.15 = (f32[6144]{0:T(1024)S(1)}, f32[6144]{0:T(1024)}, u32[]{:S(2)}) copy-start(f32[6144]{0:T(1024)} %get-tuple-element.25) | copy-start | bytes 73732
  399.8 34.3 %copy-start.16 = (f32[6144]{0:T(1024)S(1)}, f32[6144]{0:T(1024)}, u32[]{:S(2)}) copy-start(f32[6144]{0:T(1024)} %get-tuple-element.26) | copy-start | bytes 73732
  399.8 80.0 %copy-start.9 = (bf16[192,768]{1,0:T(8,128)(2,1)S(1)}, bf16[192,768]{1,0:T(8,128)(2,1)}, u32[]{:S(2)}) copy-start(bf16[192,768]{1,0:T(8,128)(2,1)} %param.18) | copy-start | bytes 884740
  399.8 80.0 %copy-start.18 = (s32[192]{0:T(256)S(1)}, s32[192]{0:T(256)}, u32[]{:S(2)}) copy-start(s32[192]{0:T(256)} %copy-done.17) | copy-start | bytes 2308
  483.7 40.7 %all-to-all-start.1 = ((bf16[8,192,768]{2,1,0:T(8,128)(2,1)}), bf16[8,192,768]{2,1,0:T(8,128)(2,1)S(1)}, u32[]{:S(2)}, u32[]{:S(2)}) async-start(bf16[8,192,768]{2,1,0:T(8,128)(2,1)} %stack.2), calls=%async_computation.2 | async-start | bytes 4718592 | tf_op jit(solution)/shard_map/all_to_all | solution.py:108
  487.3 103.5 %all-gather.7.cloned.1.call-start = ((), (), s32[]{:S(2)}) async-start(), calls=%async_computation.5 | async-start | bytes 2654208 | tf_op jit(solution)/shard_map/all_gather | solution.py:102
  524.4 1.4 copy-start.4
  525.8 19.2 %copy-start.3 = (bf16[6144,128]{1,0:T(8,128)(2,1)S(1)}, bf16[6144,128]{1,0:T(8,128)(2,1)}, u32[]{:S(2)}) copy-start(bf16[6144,128]{1,0:T(8,128)(2,1)} %all-gather.9.cloned.1.call-done) | copy-start | bytes 4718596
  547.4 10.4 %copy-start.2 = (bf16[6144,128]{1,0:T(8,128)(2,1)S(1)}, bf16[6144,128]{1,0:T(8,128)(2,1)}, u32[]{:S(2)}) copy-start(bf16[6144,128]{1,0:T(8,128)(2,1)} %all-gather.5.cloned.1.call-done) | copy-start | bytes 4718596
  549.1 17.4 %all-to-all-start.2 = ((f32[32,1,384]{2,1,0:T(1,128)}), f32[32,1,384]{2,1,0:T(1,128)S(1)}, u32[]{:S(2)}, u32[]{:S(2)}) async-start(f32[32,1,384]{2,1,0:T(1,128)} %reshape.226), calls=%async_computation.3 | async-start | bytes 98304 | tf_op jit(solution)/shard_map/all_to_all | solution.py:122
Sparse Core Ops, SparseCore 0:
  11.1 55.2 all-gather.4
  69.5 50.4 all-gather.8
  123.4 247.3 all-reduce.7
  373.4 106.3 reduce-scatter.1
  482.2 62.7 all-gather.10
  546.8 44.0 all-gather.6
